TPU v7x, 256 devices: a whole 4x4x8 slice. The times are simulated.
256 devices in a mesh: dp: 4 (over z_lo), ctx: 64 (over z_hi, x, y, core).
Axes of the slice: x: 4, y: 4, z: 8 (z_hi: 2, z_lo: 4; z = z_hi * 4 + z_lo), core: 2. Of those that a mesh axis runs over, the one named last changes fastest.
Arguments:
- inputs: bfloat16 [4, 16384, 4096], P('dp', 'ctx'), may hold values from -16 to 16
- value_weight: bfloat16 [4096, 512], P('ctx'), may hold values from -0.09375 to 0.09375
- query_states: bfloat16 [4, 16384, 2048], P('dp', 'ctx'), may hold values from -40 to 40
- key_states: bfloat16 [4, 16384, 512], P('dp', 'ctx'), may hold values from -6 to 6
- value_states: bfloat16 [4, 16384, 512], P('dp', 'ctx'), may hold values from -6 to 6
- attention_out: bfloat16 [4, 16384, 2048], P('dp', 'ctx'), may hold values from -4 to 4
- out_grad: bfloat16 [4, 16384, 2048], P('dp', 'ctx'), may hold values from -6 to 6
- segment_ids: int32 [4, 16384], P('dp', 'ctx'), may hold values from 0 to 31, never falling along the last dimension, each value on 1 to 4096 neighbouring positions
Outputs:
- query_grad: bfloat16 [4, 16384, 2048], P('dp', 'ctx')
- key_grad: bfloat16 [4, 16384, 512], P('dp', 'ctx')
- input_grad: bfloat16 [4, 16384, 4096], P('dp', 'ctx')
- weight_grad: float32 [4096, 512], P('ctx')
Inputs may be any that keep to these rules, and one draw needn't show every extreme that they name: `segment_ids`: along each sequence the ids never fall; each record holds 1 to 4096 tokens and one holds exactly 4096.
All inputs are finite; a program needn't handle non-finite values.
Results may differ from a plain program's by a relative error of at most 0.0057.
Values may be sent and summed in bfloat16 or wider, within the bound.
A program may use at most 128 MiB of HBM per device.

v0:
```python
import math
import jax
import jax.numpy as jnp
from jax import lax
from jax.sharding import PartitionSpec as P

HQ = 16
KVH = 4
DH = 128
W = 2048


def carried_in(value, axis, combine, identity):
    peers, here = (lax.axis_size(axis), lax.axis_index(axis))
    everything = jax.tree.map(lambda part: lax.all_gather(part, axis), value)
    start = jax.tree.map(
        lambda part, zero: jnp.broadcast_to(jnp.asarray(zero, part.dtype), part.shape),
        value,
        identity,
    )

    def turn(k, before):
        reached = k < here
        new = combine(before, jax.tree.map(lambda part: part[k], everything))
        return jax.tree.map(lambda a, b: jnp.where(reached, a, b), new, before)

    return lax.fori_loop(0, peers, turn, start)


def passed_along(block, axis, distance):
    devices = range(lax.axis_size(axis))
    route = [(i - distance, i) for i in devices if i - distance in devices]
    return lax.ppermute(block, axis, route)


def link_records(earlier, later):
    first_early, last_early, start_early, whole_early, empty_early = earlier
    first_late, last_late, start_late, whole_late, empty_late = later
    joined = last_early == first_late
    start_merged = jnp.where((whole_late == 1) & joined, start_early, start_late)
    whole_merged = jnp.where((whole_early == 1) & (whole_late == 1) & joined, 1, 0).astype(
        jnp.int32
    )
    merged = (first_early, last_late, start_merged, whole_merged, jnp.zeros_like(empty_early))
    return tuple(
        (
            jnp.where(
                empty_early == 1, late_item, jnp.where(empty_late == 1, early_item, merged_item)
            )
            for early_item, late_item, merged_item in zip(earlier, later, merged)
        )
    )


def attend_group(operands, live_mask, factor):
    query_group, key_group, value_group, grad_group, output_group = operands
    scores = (
        jnp.einsum("gqd,kd->gqk", query_group, key_group, preferred_element_type=jnp.float32)
        * factor
    )
    scores = jnp.where(live_mask[None], scores, -1e30)
    row_max = jnp.max(scores, axis=-1, keepdims=True)
    exp_score = jnp.exp(scores - row_max)
    prob_full = exp_score / jnp.sum(exp_score, axis=-1, keepdims=True)
    prob_low = prob_full.astype(jnp.bfloat16)
    row_delta = jnp.sum(
        grad_group.astype(jnp.float32) * output_group.astype(jnp.float32), axis=-1, keepdims=True
    )
    prob_grad = jnp.einsum(
        "gqd,kd->gqk", grad_group, value_group, preferred_element_type=jnp.float32
    )
    score_grad = (prob_full * (prob_grad - row_delta)).astype(jnp.bfloat16)
    query_part = (
        jnp.einsum("gqk,kd->gqd", score_grad, key_group, preferred_element_type=jnp.float32)
        * factor
    )
    key_part = (
        jnp.einsum("gqk,gqd->kd", score_grad, query_group, preferred_element_type=jnp.float32)
        * factor
    )
    value_part = jnp.einsum("gqk,gqd->kd", prob_low, grad_group, preferred_element_type=jnp.float32)
    return (query_part, key_part, value_part)


def attend_tail(factor, operands):
    query_heads, key_heads, value_heads, grad_heads, output_heads, live_mask = operands
    query_part, key_part, value_part = lax.map(
        lambda head_parts: attend_group(head_parts, live_mask, factor),
        (query_heads, key_heads, value_heads, grad_heads, output_heads),
    )
    return (query_part, key_part, value_part)


def on_device(
    inputs,
    value_weight,
    query_states,
    key_states,
    value_states,
    attention_out,
    out_grad,
    segment_ids,
):
    tok_rows = query_states.shape[1]
    span_blocks = W // tok_rows
    group_size = HQ // KVH
    width_kv = KVH * DH
    factor = 1.0 / math.sqrt(DH)
    window_rows = (span_blocks + 1) * tok_rows
    input_rows = inputs[0]
    values = value_states[0]
    seg_local = segment_ids[0]
    device_index = lax.axis_index("ctx")
    offset = device_index * tok_rows
    before = jnp.sum((seg_local[None, :] < seg_local[:, None]).astype(jnp.int32), axis=1)
    first_id = seg_local[0]
    last_id = seg_local[-1]
    summary = (
        first_id,
        last_id,
        offset + before[-1],
        (first_id == last_id).astype(jnp.int32),
        jnp.zeros((), jnp.int32),
    )
    identity = tuple((jnp.full((), filler, jnp.int32) for filler in (0, 0, 0, 1, 1)))
    prior = carried_in(summary, "ctx", link_records, identity)
    carried = (before == 0) & (prior[4] == 0) & (prior[1] == first_id)
    starts = jnp.where(carried, prior[2], offset + before)
    kv_block = jnp.stack([key_states[0], values])
    blank_window = jnp.zeros((2, window_rows, width_kv), jnp.bfloat16)
    blank_window = lax.dynamic_update_slice_in_dim(
        blank_window, kv_block, span_blocks * tok_rows, 1
    )

    def pass_on(hop_number, carry):
        moving, filled = carry
        moving = passed_along(moving, "ctx", 1)
        filled = lax.dynamic_update_slice_in_dim(
            filled, moving, (span_blocks - hop_number) * tok_rows, 1
        )
        return (moving, filled)

    window = lax.fori_loop(1, span_blocks + 1, pass_on, (kv_block, blank_window))[1]
    key_base = offset - span_blocks * tok_rows
    key_pos = key_base + jnp.arange(window_rows, dtype=jnp.int32)
    query_pos = offset + jnp.arange(tok_rows, dtype=jnp.int32)
    live_mask = (
        (key_pos[None, :] >= starts[:, None])
        & (key_pos[None, :] <= query_pos[:, None])
        & (key_pos[None, :] > query_pos[:, None] - W)
    )
    query_heads = query_states[0].reshape(tok_rows, KVH, group_size, DH).transpose(1, 2, 0, 3)
    grad_heads = out_grad[0].reshape(tok_rows, KVH, group_size, DH).transpose(1, 2, 0, 3)
    output_heads = attention_out[0].reshape(tok_rows, KVH, group_size, DH).transpose(1, 2, 0, 3)
    key_heads = window[0].reshape(window_rows, KVH, DH).transpose(1, 0, 2)
    value_heads = window[1].reshape(window_rows, KVH, DH).transpose(1, 0, 2)
    operands = (query_heads, key_heads, value_heads, grad_heads, output_heads, live_mask)
    query_part, key_part, value_part = attend_tail(factor, operands)
    query_grad = query_part.transpose(2, 0, 1, 3).reshape(1, tok_rows, HQ * DH).astype(jnp.bfloat16)
    grads = jnp.stack(
        [
            key_part.transpose(1, 0, 2).reshape(window_rows, width_kv),
            value_part.transpose(1, 0, 2).reshape(window_rows, width_kv),
        ]
    )

    def return_step(hop_number, carried_sum):
        moved = passed_along(carried_sum, "ctx", -1)
        return moved + lax.dynamic_slice_in_dim(grads, hop_number * tok_rows, tok_rows, 1)

    totals = lax.fori_loop(1, span_blocks + 1, return_step, grads[:, :tok_rows])
    key_grad = totals[0].astype(jnp.bfloat16)[None]
    value_delta = totals[1].astype(jnp.bfloat16)
    input_grad = jnp.einsum(
        "tk,rk->tr",
        value_delta,
        lax.all_gather(value_weight, "ctx", axis=0, tiled=True),
        preferred_element_type=jnp.float32,
    )
    input_grad = input_grad.astype(jnp.bfloat16)[None]
    weight_share = lax.psum_scatter(
        jnp.einsum("tr,tk->rk", input_rows, value_delta, preferred_element_type=jnp.float32),
        "ctx",
        scatter_dimension=0,
        tiled=True,
    )
    weight_grad = lax.psum(weight_share, "dp")
    return (query_grad, key_grad, input_grad, weight_grad)


def solution(mesh):
    placed = (
        P("dp", "ctx", None),
        P("ctx", None),
        P("dp", "ctx", None),
        P("dp", "ctx", None),
        P("dp", "ctx", None),
        P("dp", "ctx", None),
        P("dp", "ctx", None),
        P("dp", "ctx"),
    )
    return jax.shard_map(
        on_device,
        mesh=mesh,
        in_specs=placed,
        out_specs=(
            P("dp", "ctx", None),
            P("dp", "ctx", None),
            P("dp", "ctx", None),
            P("ctx", None),
        ),
        check_vma=False,
    )
```

profile of v0, /device:TPU:2, one launch (start us, length us, event | category | flops | bytes accessed | tf_op | source)
XLA Modules:
  0.0 1700.2 jit_solution(13102222631023237591)
XLA Ops:
  18.7 24.4 %all-reduce.6 = (s32[64]{0:T(128)S(1)}, s32[64]{0:T(128)S(1)}, s32[64]{0:T(128)S(1)}, s32[64]{0:T(128)S(1)}, s32[64]{0:T(128)S(1)}) all-reduce(s32[64]{0:T(128)S(1)} %bitcast_dynamic-update-slice_fusion.1, s32[64]{0:T(128)S(1)} %dynamic-update-slice.1, s32[64]{0:T(128)S(1)} %dynamic-update-slice.2, ...), channel_id=2, replica_groups=mesh['dp'=4,'ctx'=64] {'ctx'}, use_global_device_ids=true, to_apply=%add.1 | all-reduce | flops 320 | bytes 2560 | tf_op jit(solution)/shard_map/all_gather | solution.py:15
  43.1 521.7 %while.60 = (s32[]{:T(128)}, s32[]{:T(128)}, s32[]{:T(128)}, s32[]{:T(128)}, s32[]{:T(128)}, /*index=5*/s32[64]{0:T(128)S(1)}, s32[64]{0:T(128)S(1)}, s32[64]{0:...) while((s32[]{:T(128)}, s32[]{:T(128)}, s32[]{:T(128)}, ...), condition=%wide.region_4.5_spmd, body=%wide.region_3.4_spmd.sunk | while | flops 18 | bytes 363 | solution.py:27
  567.3 2.5 dynamic_update_slice.21
  569.8 107.9 %while.61 = (s32[]{:T(128)}, bf16[2,256,512]{2,1,0:T(8,128)(2,1)S(1)}, bf16[2,2304,512]{2,1,0:T(8,128)(2,1)}, s32[]{:T(128)}, s32[]{:T(128)}, /*index=5*/s32[]{:T(128)}, s32[]{:T(128)}, s32[]{:T(128)}) while((s32[]{:T(128)}, bf16[2,256,512]{2,1,0:T(8,128)(2,1)S(1)}, bf16[2,2304,512]{2,1,0:T(8,128)(2,1)}, s32[]{:T(128)}, s32[]{:T(128)}, ...), condition=%wide.region_1.2_spmd, body=%wide.region_0.0_spmd.sunk | while | flops 7 | bytes 4194491 | solution.py:143
  571.7 10.7 collective-permute-done
  585.2 10.7 collective-permute-done
  598.7 10.7 collective-permute-done
  612.2 10.7 collective-permute-done
  625.7 10.7 collective-permute-done
  639.2 10.7 collective-permute-done
  652.7 10.7 collective-permute-done
  666.1 10.7 collective-permute-done
  677.7 6.7 copy.55
  684.4 4.9 fusion.82
  695.2 144.7 %while.63 = (s32[]{:T(128)}, bf16[4,4,256,128]{3,2,1,0:T(8,128)(2,1)}, f32[4,2304,128]{1,2,0:T(8,128)}, f32[4,2304,128]{1,2,0:T(8,128)}, bf16[4,4,256,128]{2,3,1...) while((s32[]{:T(128)}, ...), condition=%wide.region_9.10_spmd.clone, body=%wide.region_5.9_spmd.clone.sunk | while | flops 3658453504 | bytes 69966016 | solution.py:87
  697.8 8.6 fusion.117
  706.4 5.4 multiply_convert_fusion.2
  714.0 3.4 fusion.119
  720.1 4.6 fusion.118
  724.7 6.8 fusion.120
  733.9 8.6 fusion.117
  742.5 5.4 multiply_convert_fusion.2
  750.1 3.4 fusion.119
  756.2 4.6 fusion.118
  760.8 6.8 fusion.120
  770.1 8.6 fusion.117
  778.6 5.4 multiply_convert_fusion.2
  786.2 3.4 fusion.119
  792.4 4.6 fusion.118
  796.9 6.8 fusion.120
  806.2 8.6 fusion.117
  814.7 5.4 multiply_convert_fusion.2
  822.3 3.4 fusion.119
  828.5 4.6 fusion.118
  833.1 6.8 fusion.120
  839.9 8.8 pad_maximum_fusion
  850.3 163.5 %while.62 = (s32[]{:T(128)}, f32[2,256,512]{2,1,0:T(8,128)}, f32[2,2304,512]{1,2,0:T(8,128)}, s32[]{:T(128)}, s32[]{:T(128)}, /*index=5*/s32[]{:T(128)}, s32[]{:T(128)}) while((s32[]{:T(128)}, f32[2,256,512]{2,1,0:T(8,128)}, f32[2,2304,512]{1,2,0:T(8,128)}, s32[]{:T(128)}, s32[]{:T(128)}, /*index=5*/s32[]{:T(128)}, s32[]{:T(128)}) %tuple.122), condition=%wide.region_11.12_spmd, body=%wide.region_10.11_spmd.sunk | while | flops 262150 | bytes 11534503 | solution.py:171
  856.0 8.8 collective-permute-done.1
  864.8 2.4 add.167
  867.2 5.9 collective-permute-start.1
  877.0 8.8 collective-permute-done.1
  885.7 2.4 add.167
  888.1 5.9 collective-permute-start.1
  897.9 8.8 collective-permute-done.1
  906.7 2.4 add.167
  909.1 5.9 collective-permute-start.1
  918.8 8.8 collective-permute-done.1
  927.6 2.4 add.167
  930.0 5.9 collective-permute-start.1
  939.8 8.8 collective-permute-done.1
  950.9 5.9 collective-permute-start.1
  960.7 8.8 collective-permute-done.1
  971.9 5.9 collective-permute-start.1
  981.6 8.8 collective-permute-done.1
  990.4 2.4 add.167
  992.8 5.9 collective-permute-start.1
  1002.6 8.8 collective-permute-done.1
  1011.4 2.4 add.167
  1013.8 5.5 convolution_bitcast_fusion.1
  1019.3 9.0 copy.72
  1034.6 484.9 %reduce-scatter.4.cloned.1.call-done = f32[64,512]{1,0:T(8,128)} async-done(((f32[4096,512]{1,0:T(8,128)}), f32[64,512]{1,0:T(8,128)}) %reduce-scatter.4.cloned.1.call-update) | async-done | bytes 131088
  1521.2 123.7 %all-gather.4.cloned.1.call-done = bf16[4096,512]{1,0:T(8,128)(2,1)} async-done(((bf16[64,512]{1,0:T(8,128)(2,1)}), bf16[4096,512]{1,0:T(8,128)(2,1)}) %all-gather.4.cloned.1.call-update) | async-done | bytes 4194320 | tf_op jit(solution)/shard_map/all_gather | solution.py:177
  1644.9 5.0 fusion.71
  1649.9 42.0 %all-reduce.9.cloned.1.call-done = f32[64,512]{0,1:T(8,128)} async-done(((f32[64,512]{0,1:T(8,128)}), f32[64,512]{0,1:T(8,128)}) %all-reduce.9.cloned.1.call-update) | async-done | bytes 131088 | tf_op jit(solution)/shard_map/psum | solution.py:187
  (453 shorter events, 312.4 us)
Async XLA Ops:
  7.2 1006.6 %copy-start = (bf16[1,256,4096]{2,1,0:T(8,128)(2,1)S(1)}, bf16[1,256,4096]{2,1,0:T(8,128)(2,1)}, u32[]{:S(2)}) copy-start(bf16[1,256,4096]{2,1,0:T(8,128)(2,1)} %param.16) | copy-start | bytes 6291460
  7.2 1512.3 %reduce-scatter.4.cloned.1.call-start = ((), (), s32[]{:S(2)}) async-start(), calls=%async_computation.3 | async-start | bytes 8519680
  569.8 12.6 collective-permute-start
  583.3 12.6 collective-permute-start
  596.8 12.6 collective-permute-start
  610.3 12.6 collective-permute-start
  623.8 12.6 collective-permute-start
  637.3 12.6 collective-permute-start
  650.7 12.6 collective-permute-start
  664.2 12.6 collective-permute-start
  684.4 4.9 copy-start.5
  697.8 8.6 copy-start.4
  711.9 2.1 copy-start.1
  733.9 8.6 copy-start.4
  747.9 2.1 copy-start.1
  770.1 8.6 copy-start.4
  784.1 2.1 copy-start.1
  806.2 8.6 copy-start.4
  820.2 2.1 copy-start.1
  839.9 8.9 copy-start.2
  839.9 9.0 copy-start.3
  850.3 14.5 collective-permute-start.1
  867.2 18.5 %collective-permute-start.1 = (f32[2,256,512]{2,1,0:T(8,128)}, f32[2,256,512]{2,1,0:T(8,128)}, u32[]{:S(2)}, u32[]{:S(2)}) collective-permute-start(f32[2,256,512]{2,1,0:T(8,128)} %get-tuple-element.833), channel_id=1, source_target_pairs={{1,0},{2,1},{3,2},{4,3},{5,4},{6,5},{7,6},{8,7},{9,8},{10,9},{11,1... | collective-permute-start | bytes 3145736 | tf_op jit(solution)/shard_map/while/body/eval_jaxpr/ppermute | solution.py:33
  888.1 18.5 %collective-permute-start.1 = (f32[2,256,512]{2,1,0:T(8,128)}, f32[2,256,512]{2,1,0:T(8,128)}, u32[]{:S(2)}, u32[]{:S(2)}) collective-permute-start(f32[2,256,512]{2,1,0:T(8,128)} %get-tuple-element.833), channel_id=1, source_target_pairs={{1,0},{2,1},{3,2},{4,3},{5,4},{6,5},{7,6},{8,7},{9,8},{10,9},{11,1... | collective-permute-start | bytes 3145736 | tf_op jit(solution)/shard_map/while/body/eval_jaxpr/ppermute | solution.py:33
  909.1 18.5 %collective-permute-start.1 = (f32[2,256,512]{2,1,0:T(8,128)}, f32[2,256,512]{2,1,0:T(8,128)}, u32[]{:S(2)}, u32[]{:S(2)}) collective-permute-start(f32[2,256,512]{2,1,0:T(8,128)} %get-tuple-element.833), channel_id=1, source_target_pairs={{1,0},{2,1},{3,2},{4,3},{5,4},{6,5},{7,6},{8,7},{9,8},{10,9},{11,1... | collective-permute-start | bytes 3145736 | tf_op jit(solution)/shard_map/while/body/eval_jaxpr/ppermute | solution.py:33
  930.0 18.5 %collective-permute-start.1 = (f32[2,256,512]{2,1,0:T(8,128)}, f32[2,256,512]{2,1,0:T(8,128)}, u32[]{:S(2)}, u32[]{:S(2)}) collective-permute-start(f32[2,256,512]{2,1,0:T(8,128)} %get-tuple-element.833), channel_id=1, source_target_pairs={{1,0},{2,1},{3,2},{4,3},{5,4},{6,5},{7,6},{8,7},{9,8},{10,9},{11,1... | collective-permute-start | bytes 3145736 | tf_op jit(solution)/shard_map/while/body/eval_jaxpr/ppermute | solution.py:33
  950.9 18.5 %collective-permute-start.1 = (f32[2,256,512]{2,1,0:T(8,128)}, f32[2,256,512]{2,1,0:T(8,128)}, u32[]{:S(2)}, u32[]{:S(2)}) collective-permute-start(f32[2,256,512]{2,1,0:T(8,128)} %get-tuple-element.833), channel_id=1, source_target_pairs={{1,0},{2,1},{3,2},{4,3},{5,4},{6,5},{7,6},{8,7},{9,8},{10,9},{11,1... | collective-permute-start | bytes 3145736 | tf_op jit(solution)/shard_map/while/body/eval_jaxpr/ppermute | solution.py:33
  971.9 18.5 %collective-permute-start.1 = (f32[2,256,512]{2,1,0:T(8,128)}, f32[2,256,512]{2,1,0:T(8,128)}, u32[]{:S(2)}, u32[]{:S(2)}) collective-permute-start(f32[2,256,512]{2,1,0:T(8,128)} %get-tuple-element.833), channel_id=1, source_target_pairs={{1,0},{2,1},{3,2},{4,3},{5,4},{6,5},{7,6},{8,7},{9,8},{10,9},{11,1... | collective-permute-start | bytes 3145736 | tf_op jit(solution)/shard_map/while/body/eval_jaxpr/ppermute | solution.py:33
  992.8 18.5 %collective-permute-start.1 = (f32[2,256,512]{2,1,0:T(8,128)}, f32[2,256,512]{2,1,0:T(8,128)}, u32[]{:S(2)}, u32[]{:S(2)}) collective-permute-start(f32[2,256,512]{2,1,0:T(8,128)} %get-tuple-element.833), channel_id=1, source_target_pairs={{1,0},{2,1},{3,2},{4,3},{5,4},{6,5},{7,6},{8,7},{9,8},{10,9},{11,1... | collective-permute-start | bytes 3145736 | tf_op jit(solution)/shard_map/while/body/eval_jaxpr/ppermute | solution.py:33
  1028.4 616.6 %all-gather.4.cloned.1.call-start = ((), (), s32[]{:S(2)}) async-start(), calls=%async_computation.1 | async-start | bytes 4259840 | tf_op jit(solution)/shard_map/all_gather | solution.py:177
  1029.1 662.8 %all-reduce.9.cloned.1.call-start = ((), (), s32[]{:S(2)}) async-start(), calls=%async_computation.2 | async-start | bytes 524288 | tf_op jit(solution)/shard_map/psum | solution.py:187
Sparse Core Ops, SparseCore 0:
  1028.5 490.9 reduce-scatter.3
  1523.1 121.7 all-gather.3
  1647.5 44.3 all-reduce.8
where the time goes:
time: 1710 us; the launch traced here: 1700 us
  waiting for transfers between devices  807 us (47%)
  loops' own time  327 us (19%)
  local copies, waits for them, and re-layouts  308 us (18%)
  matrix products  126 us (7%)
  starting transfers between devices  58.7 us (3%)
  other arithmetic  33.3 us (2%)
  blocking collectives  24.4 us (1%)
    unnamed x4, waiting for transfers between devices  486 us
    another operation x1, loops' own time, carried_in(): return lax.fori_loop(0, peers, turn, start)  327 us
    dynamic_slice x320, local copies, waits for them, and re-layouts, turn(): new = combine(before, jax.tree.map(lambda part: part[k], everything))  195 us
    ppermute x16, waiting for transfers between devices, passed_along(): return lax.ppermute(block, axis, route)  156 us
    all_gather x1, waiting for transfers between devices, on_device(): lax.all_gather(value_weight, 'ctx', axis=0, tiled=True)  124 us
    ppermute x16, starting transfers between devices, passed_along(): return lax.ppermute(block, axis, route)  58.6 us
    psum x1, waiting for transfers between devices, on_device(): weight_grad = lax.psum(weight_share, 'dp')  42 us
    sub x4, matrix products, attend_group(): exp_score = jnp.exp(scores - row_max)  34.2 us
  transfers between devices with their start and end apart: 19, of which 19 were waited for; matrix products, arithmetic and copies ran while one was open for 3% of the time, Pallas kernels for 0%

commit v1 on v0

--- a/solution.py
+++ b/solution.py
@@ -184,7 +184,8 @@
         scatter_dimension=0,
         tiled=True,
     )
-    weight_grad = lax.psum(weight_share, "dp")
+    frame_out = lax.all_gather(weight_share, axis_name="dp")
+    weight_grad = jnp.sum(frame_out, axis=0)
     return (query_grad, key_grad, input_grad, weight_grad)
 
 

time: 1710 us -> 1570 us (0.918)
  the two profiles are of different devices: /device:TPU:2 before, /device:TPU:0 now
where the time goes in v1:
time: 1570 us
  waiting for transfers between devices  659 us (42%)
  loops' own time  315 us (20%)
  local copies, waits for them, and re-layouts  303 us (19%)
  matrix products  126 us (8%)
  starting transfers between devices  73.1 us (5%)
  blocking collectives  38.8 us (2%)
  other arithmetic  34.6 us (2%)
  between operations  16.8 us (1%)
    reduce_scatter x1, waiting for transfers between devices, on_device(): lax.psum_scatter(jnp.einsum('tr,tk->rk', input_rows, value_delta, preferr...  560 us
    another operation x1, loops' own time, carried_in(): return lax.fori_loop(0, peers, turn, start)  315 us
    dynamic_slice x320, local copies, waits for them, and re-layouts, turn(): new = combine(before, jax.tree.map(lambda part: part[k], everything))  194 us
    ppermute x16, waiting for transfers between devices, passed_along(): return lax.ppermute(block, axis, route)  98 us
    ppermute x16, starting transfers between devices, passed_along(): return lax.ppermute(block, axis, route)  73 us
    sub x4, matrix products, attend_group(): exp_score = jnp.exp(scores - row_max)  34.2 us
  transfers between devices with their start and end apart: 18, of which 17 were waited for; matrix products, arithmetic and copies ran while one was open for 29% of the time, Pallas kernels for 0%

profile of v1, /device:TPU:0, one launch (start us, length us, event | category | flops | bytes accessed | tf_op | source)
XLA Modules:
  0.0 1565.6 jit_solution(8038970534555572962)
XLA Ops:
  19.0 24.0 %all-reduce.6 = (s32[64]{0:T(128)S(1)}, s32[64]{0:T(128)S(1)}, s32[64]{0:T(128)S(1)}, s32[64]{0:T(128)S(1)}, s32[64]{0:T(128)S(1)}) all-reduce(s32[64]{0:T(128)S(1)} %bitcast_dynamic-update-slice_fusion.1, s32[64]{0:T(128)S(1)} %dynamic-update-slice.1, s32[64]{0:T(128)S(1)} %dynamic-update-slice.2, ...), channel_id=2, replica_groups=mesh['dp'=4,'ctx'=64] {'ctx'}, use_global_device_ids=true, to_apply=%add.1 | all-reduce | flops 320 | bytes 2560 | tf_op jit(solution)/shard_map/all_gather | solution.py:15
  43.0 508.5 %while.60 = (s32[]{:T(128)}, s32[]{:T(128)}, s32[]{:T(128)}, s32[]{:T(128)}, s32[]{:T(128)}, /*index=5*/s32[64]{0:T(128)S(1)}, s32[64]{0:T(128)S(1)}, s32[64]{0:...) while((s32[]{:T(128)}, s32[]{:T(128)}, s32[]{:T(128)}, ...), condition=%wide.region_4.5_spmd, body=%wide.region_3.4_spmd.sunk | while | flops 18 | bytes 363 | solution.py:27
  554.2 2.5 dynamic_update_slice.21
  556.6 81.9 %while.61 = (s32[]{:T(128)}, bf16[2,256,512]{2,1,0:T(8,128)(2,1)S(1)}, bf16[2,2304,512]{2,1,0:T(8,128)(2,1)}, s32[]{:T(128)}, s32[]{:T(128)}, /*index=5*/s32[]{:T(128)}, s32[]{:T(128)}, s32[]{:T(128)}) while((s32[]{:T(128)}, bf16[2,256,512]{2,1,0:T(8,128)(2,1)S(1)}, bf16[2,2304,512]{2,1,0:T(8,128)(2,1)}, s32[]{:T(128)}, s32[]{:T(128)}, ...), condition=%wide.region_1.2_spmd, body=%wide.region_0.0_spmd.sunk | while | flops 7 | bytes 4194491 | solution.py:143
  560.3 7.5 collective-permute-start
  570.2 9.0 collective-permute-start
  581.6 9.0 collective-permute-start
  593.0 9.0 collective-permute-start
  604.4 9.0 collective-permute-start
  615.7 9.0 collective-permute-start
  627.1 9.0 collective-permute-start
  638.5 6.8 copy.54
  645.3 5.0 fusion.82
  656.1 144.7 %while.63 = (s32[]{:T(128)}, bf16[4,4,256,128]{3,2,1,0:T(8,128)(2,1)}, f32[4,2304,128]{1,2,0:T(8,128)}, f32[4,2304,128]{1,2,0:T(8,128)}, bf16[4,4,256,128]{2,3,1...) while((s32[]{:T(128)}, ...), condition=%wide.region_9.10_spmd.clone, body=%wide.region_5.9_spmd.clone.sunk | while | flops 3658453504 | bytes 69966016 | solution.py:87
  658.7 8.6 fusion.117
  667.3 5.4 multiply_convert_fusion.2
  674.8 3.4 fusion.119
  681.0 4.6 fusion.118
  685.5 6.8 fusion.120
  694.8 8.6 fusion.117
  703.4 5.4 multiply_convert_fusion.2
  710.9 3.4 fusion.119
  717.1 4.6 fusion.118
  721.7 6.8 fusion.120
  731.0 8.6 fusion.117
  739.5 5.4 multiply_convert_fusion.2
  747.1 3.4 fusion.119
  753.3 4.6 fusion.118
  757.8 6.8 fusion.120
  767.1 8.6 fusion.117
  775.7 5.4 multiply_convert_fusion.2
  783.2 3.4 fusion.119
  789.4 4.6 fusion.118
  794.0 6.8 fusion.120
  803.4 8.0 pad_maximum_fusion
  811.4 146.6 %while.62 = (s32[]{:T(128)}, f32[2,256,512]{2,1,0:T(8,128)}, f32[2,2304,512]{1,2,0:T(8,128)}, s32[]{:T(128)}, s32[]{:T(128)}, /*index=5*/s32[]{:T(128)}, s32[]{:T(128)}) while((s32[]{:T(128)}, f32[2,256,512]{2,1,0:T(8,128)}, f32[2,2304,512]{1,2,0:T(8,128)}, s32[]{:T(128)}, s32[]{:T(128)}, /*index=5*/s32[]{:T(128)}, s32[]{:T(128)}) %tuple.118), condition=%wide.region_11.12_spmd, body=%wide.region_10.11_spmd.sunk | while | flops 262150 | bytes 11534503 | solution.py:171
  812.7 2.3 constant_dynamic-slice_fusion.7
  816.6 6.3 collective-permute-done.1
  822.9 2.4 add.165
  826.6 2.3 constant_dynamic-slice_fusion.7
  830.5 12.0 collective-permute-done.1
  842.5 2.4 add.165
  846.2 2.3 constant_dynamic-slice_fusion.7
  850.1 11.3 collective-permute-done.1
  861.4 2.4 add.165
  865.1 2.3 constant_dynamic-slice_fusion.7
  868.9 11.3 collective-permute-done.1
  880.2 2.4 add.165
  883.9 2.3 constant_dynamic-slice_fusion.7
  887.8 11.3 collective-permute-done.1
  899.1 2.4 add.165
  902.8 2.3 constant_dynamic-slice_fusion.7
  906.6 11.3 collective-permute-done.1
  917.9 2.4 add.165
  921.7 2.3 constant_dynamic-slice_fusion.7
  925.5 11.3 collective-permute-done.1
  936.8 2.4 add.165
  944.4 11.3 collective-permute-done.1
  955.6 2.4 add.165
  958.1 5.5 convolution_bitcast_fusion.1
  963.6 9.0 copy.71
  978.1 5.0 fusion.71
  983.0 560.2 %reduce-scatter.4.cloned.1.call-done = f32[64,512]{1,0:T(8,128)} async-done(((f32[4096,512]{1,0:T(8,128)}), f32[64,512]{1,0:T(8,128)}) %reduce-scatter.4.cloned.1.call-update) | async-done | bytes 131088 | tf_op jit(solution)/shard_map/reduce_scatter | solution.py:181
  1543.2 14.9 all-gather.2
  (446 shorter events, 294.7 us)
Async XLA Ops:
  7.2 950.9 %copy-start = (bf16[1,256,4096]{2,1,0:T(8,128)(2,1)S(1)}, bf16[1,256,4096]{2,1,0:T(8,128)(2,1)}, u32[]{:S(2)}) copy-start(bf16[1,256,4096]{2,1,0:T(8,128)(2,1)} %param.16) | copy-start | bytes 6291460
  7.2 970.9 %all-gather.5.cloned.1.call-start = ((), (), s32[]{:S(2)}) async-start(), calls=%async_computation.1 | async-start | bytes 4259840 | tf_op jit(solution)/shard_map/all_gather | solution.py:177
  7.9 1535.3 %reduce-scatter.4.cloned.1.call-start = ((), (), s32[]{:S(2)}) async-start(), calls=%async_computation.2 | async-start | bytes 8519680 | tf_op jit(solution)/shard_map/reduce_scatter | solution.py:181
  556.6 2.8 collective-permute-start
  560.3 9.0 collective-permute-start
  570.2 10.5 collective-permute-start
  581.6 10.5 collective-permute-start
  593.0 10.5 collective-permute-start
  604.4 10.5 collective-permute-start
  615.7 10.5 collective-permute-start
  627.1 10.5 collective-permute-start
  645.3 5.0 copy-start.3
  658.7 8.6 copy-start.2
  672.7 2.1 copy-start.1
  694.8 8.6 copy-start.2
  708.8 2.1 copy-start.1
  730.9 8.6 copy-start.2
  745.0 2.1 copy-start.1
  767.1 8.6 copy-start.2
  781.1 2.1 copy-start.1
  811.4 11.5 collective-permute-start.1
  825.3 17.2 %collective-permute-start.1 = (f32[2,256,512]{2,1,0:T(8,128)}, f32[2,256,512]{2,1,0:T(8,128)}, u32[]{:S(2)}, u32[]{:S(2)}) collective-permute-start(f32[2,256,512]{2,1,0:T(8,128)} %get-tuple-element.817), channel_id=1, source_target_pairs={{1,0},{2,1},{3,2},{4,3},{5,4},{6,5},{7,6},{8,7},{9,8},{10,9},{11,1... | collective-permute-start | bytes 3145736 | tf_op jit(solution)/shard_map/while/body/eval_jaxpr/ppermute | solution.py:33
  844.9 16.4 %collective-permute-start.1 = (f32[2,256,512]{2,1,0:T(8,128)}, f32[2,256,512]{2,1,0:T(8,128)}, u32[]{:S(2)}, u32[]{:S(2)}) collective-permute-start(f32[2,256,512]{2,1,0:T(8,128)} %get-tuple-element.817), channel_id=1, source_target_pairs={{1,0},{2,1},{3,2},{4,3},{5,4},{6,5},{7,6},{8,7},{9,8},{10,9},{11,1... | collective-permute-start | bytes 3145736 | tf_op jit(solution)/shard_map/while/body/eval_jaxpr/ppermute | solution.py:33
  863.8 16.4 %collective-permute-start.1 = (f32[2,256,512]{2,1,0:T(8,128)}, f32[2,256,512]{2,1,0:T(8,128)}, u32[]{:S(2)}, u32[]{:S(2)}) collective-permute-start(f32[2,256,512]{2,1,0:T(8,128)} %get-tuple-element.817), channel_id=1, source_target_pairs={{1,0},{2,1},{3,2},{4,3},{5,4},{6,5},{7,6},{8,7},{9,8},{10,9},{11,1... | collective-permute-start | bytes 3145736 | tf_op jit(solution)/shard_map/while/body/eval_jaxpr/ppermute | solution.py:33
  882.7 16.4 %collective-permute-start.1 = (f32[2,256,512]{2,1,0:T(8,128)}, f32[2,256,512]{2,1,0:T(8,128)}, u32[]{:S(2)}, u32[]{:S(2)}) collective-permute-start(f32[2,256,512]{2,1,0:T(8,128)} %get-tuple-element.817), channel_id=1, source_target_pairs={{1,0},{2,1},{3,2},{4,3},{5,4},{6,5},{7,6},{8,7},{9,8},{10,9},{11,1... | collective-permute-start | bytes 3145736 | tf_op jit(solution)/shard_map/while/body/eval_jaxpr/ppermute | solution.py:33
  901.5 16.4 %collective-permute-start.1 = (f32[2,256,512]{2,1,0:T(8,128)}, f32[2,256,512]{2,1,0:T(8,128)}, u32[]{:S(2)}, u32[]{:S(2)}) collective-permute-start(f32[2,256,512]{2,1,0:T(8,128)} %get-tuple-element.817), channel_id=1, source_target_pairs={{1,0},{2,1},{3,2},{4,3},{5,4},{6,5},{7,6},{8,7},{9,8},{10,9},{11,1... | collective-permute-start | bytes 3145736 | tf_op jit(solution)/shard_map/while/body/eval_jaxpr/ppermute | solution.py:33
  920.4 16.4 %collective-permute-start.1 = (f32[2,256,512]{2,1,0:T(8,128)}, f32[2,256,512]{2,1,0:T(8,128)}, u32[]{:S(2)}, u32[]{:S(2)}) collective-permute-start(f32[2,256,512]{2,1,0:T(8,128)} %get-tuple-element.817), channel_id=1, source_target_pairs={{1,0},{2,1},{3,2},{4,3},{5,4},{6,5},{7,6},{8,7},{9,8},{10,9},{11,1... | collective-permute-start | bytes 3145736 | tf_op jit(solution)/shard_map/while/body/eval_jaxpr/ppermute | solution.py:33
  939.2 16.4 %collective-permute-start.1 = (f32[2,256,512]{2,1,0:T(8,128)}, f32[2,256,512]{2,1,0:T(8,128)}, u32[]{:S(2)}, u32[]{:S(2)}) collective-permute-start(f32[2,256,512]{2,1,0:T(8,128)} %get-tuple-element.817), channel_id=1, source_target_pairs={{1,0},{2,1},{3,2},{4,3},{5,4},{6,5},{7,6},{8,7},{9,8},{10,9},{11,1... | collective-permute-start | bytes 3145736 | tf_op jit(solution)/shard_map/while/body/eval_jaxpr/ppermute | solution.py:33
Sparse Core Ops, SparseCore 0:
  11.7 94.1 all-gather.4
  972.8 570.4 reduce-scatter.3
